TPU v7x, 512 devices: a whole 4x4x16 slice. The times are simulated.
512 devices in a mesh: section: 8 (over x, z_hi), seq: 64 (over y, z_lo, core).
Axes of the slice: x: 4, y: 4, z: 16 (z_hi: 2, z_lo: 8; z = z_hi * 8 + z_lo), core: 2. Of those that a mesh axis runs over, the one named last changes fastest.
Arguments:
- queries: bfloat16 [8, 256, 2048], P('section', 'seq'), may hold values from -120 to 120
- keys_values: bfloat16 [8, 16384, 4096], P('section', 'seq'), may hold values from -41 to 41
- enc_len: int32 [8], P('section'), may hold values from 4096 to 16384, as said below
- order: int32 [8], replicated, may hold values from 0 to 7, each once
- d_out: bfloat16 [8, 256, 2048], P('section', 'seq'), may hold values from -6 to 6
Outputs:
- attended: bfloat16 [8, 256, 2048], P('section', 'seq')
- d_queries: bfloat16 [8, 256, 2048], P('section', 'seq')
- d_keys_values: bfloat16 [8, 16384, 4096], P('section', 'seq')
Inputs may be any that keep to these rules, and one draw needn't show every extreme that they name: Positions from enc_len on are padding; some micro-batch has exactly 16384 valid positions. `order`: every micro-batch is run by exactly one group.
All inputs are finite; a program needn't handle non-finite values.
Results may differ from a plain program's by a relative error of at most 0.0049.
Values may be sent and summed in bfloat16 or wider, within the bound.
A program may use at most 64 MiB of HBM per device.

v0:
```python
import math
import jax
import jax.numpy as jnp
from jax import lax
from jax.sharding import PartitionSpec as P

HD = 256


def combined_all(shard, axis, combine):
    everything = jax.tree.map(lambda part: lax.all_gather(part, axis), shard)
    initial = jax.tree.map(lambda part: part[0], everything)

    def step(k, so_far):
        return combine(so_far, jax.tree.map(lambda part: part[k], everything))

    return lax.fori_loop(1, lax.axis_size(axis), step, initial)


def combine_stats(first, second):
    top = jnp.maximum(first[0], second[0])
    total = first[1] * jnp.exp(first[0] - top) + second[1] * jnp.exp(second[0] - top)
    return (top, total)


def shards(queries, keys_values, enc_len, order, d_out):
    score_scale = 1.0 / math.sqrt(HD)
    section_count = lax.axis_size("section")
    my_section = lax.axis_index("section")
    seq_index = lax.axis_index("seq")
    slots = jnp.arange(section_count, dtype=jnp.int32)
    my_batch = jnp.sum(jnp.where(slots == my_section, order, 0))
    source = jnp.sum(jnp.where(order == my_section, slots, 0))
    to_batch = (slots == my_batch)[:, None, None]
    zero_bf = jnp.zeros((), jnp.bfloat16)
    query_send = jnp.where(to_batch, queries[0][None], zero_bf)
    grad_send = jnp.where(to_batch, d_out[0][None], zero_bf)
    query_recv, grad_recv = (
        lax.all_to_all(query_send, "section", split_axis=0, concat_axis=0, tiled=True),
        lax.all_to_all(grad_send, "section", split_axis=0, concat_axis=0, tiled=True),
    )
    query_local = jnp.sum(query_recv, axis=0, dtype=jnp.bfloat16)
    grad_local = jnp.sum(grad_recv, axis=0, dtype=jnp.bfloat16)
    query_all, grad_all = (
        lax.all_gather(query_local, "seq", axis=0, tiled=True),
        lax.all_gather(grad_local, "seq", axis=0, tiled=True),
    )
    local_rows = keys_values.shape[1]
    tq_rows = queries.shape[1]
    attn_width = keys_values.shape[2] // 2
    head_count = attn_width // HD
    memory = keys_values[0]
    key_heads = memory[:, :attn_width].reshape(local_rows, head_count, HD)
    value_heads = memory[:, attn_width:].reshape(local_rows, head_count, HD)
    query_heads = query_all.reshape(-1, head_count, HD)
    grad_heads = grad_all.reshape(-1, head_count, HD)
    length = enc_len[0]
    first_key = seq_index * local_rows
    key_valid = jnp.arange(local_rows, dtype=jnp.int32) + first_key < length
    scores = (
        jnp.einsum("ihd,jhd->hij", query_heads, key_heads, preferred_element_type=jnp.float32)
        * score_scale
    )
    scores = jnp.where(key_valid[None, None, :], scores, -jnp.inf)
    local_max = jnp.maximum(jnp.max(scores, axis=-1), -1e30)
    local_sum = jnp.sum(jnp.exp(scores - local_max[..., None]), axis=-1)
    whole_max, whole_sum = combined_all((local_max, local_sum), "seq", combine_stats)
    probabilities = jnp.exp(scores - whole_max[..., None]) / whole_sum[..., None]
    weights = probabilities.astype(jnp.bfloat16)
    result = jnp.einsum("hij,jhd->ihd", weights, value_heads, preferred_element_type=jnp.float32)
    attended_sum = lax.psum_scatter(
        result.reshape(tq_rows * lax.axis_size("seq"), attn_width),
        "seq",
        scatter_dimension=0,
        tiled=True,
    )
    dprobs = jnp.einsum("ihd,jhd->hij", grad_heads, value_heads, preferred_element_type=jnp.float32)
    delta = lax.psum(jnp.sum(probabilities * dprobs, axis=-1), "seq")
    dscores = (probabilities * (dprobs - delta[..., None]) * score_scale).astype(jnp.bfloat16)
    result = jnp.einsum("hij,jhd->ihd", dscores, key_heads, preferred_element_type=jnp.float32)
    query_sum = lax.psum_scatter(
        result.reshape(tq_rows * lax.axis_size("seq"), attn_width),
        "seq",
        scatter_dimension=0,
        tiled=True,
    )
    attended = attended_sum.astype(jnp.bfloat16)
    d_queries = query_sum.astype(jnp.bfloat16)
    key_grad = jnp.einsum("hij,ihd->jhd", dscores, query_heads, preferred_element_type=jnp.float32)
    value_grad = jnp.einsum("hij,ihd->jhd", weights, grad_heads, preferred_element_type=jnp.float32)
    joined = jnp.concatenate(
        [key_grad.reshape(local_rows, attn_width), value_grad.reshape(local_rows, attn_width)],
        axis=1,
    )
    d_memory = joined.astype(jnp.bfloat16)
    to_source = (slots == source)[:, None, None]
    attended_back = jnp.where(to_source, attended[None], zero_bf)
    queries_back = jnp.where(to_source, d_queries[None], zero_bf)
    attended_home, queries_home = (
        lax.all_to_all(attended_back, "section", split_axis=0, concat_axis=0, tiled=True),
        lax.all_to_all(queries_back, "section", split_axis=0, concat_axis=0, tiled=True),
    )
    attended_out = jnp.sum(attended_home, axis=0, dtype=jnp.bfloat16)
    queries_out = jnp.sum(queries_home, axis=0, dtype=jnp.bfloat16)
    return (attended_out[None], queries_out[None], d_memory[None])


def solution(mesh):
    placed = (
        P("section", "seq", None),
        P("section", "seq", None),
        P("section"),
        P(),
        P("section", "seq", None),
    )
    return jax.shard_map(
        shards,
        mesh=mesh,
        in_specs=placed,
        out_specs=(P("section", "seq", None), P("section", "seq", None), P("section", "seq", None)),
        check_vma=False,
    )
```

profile of v0, /device:TPU:2, one launch (start us, length us, event | category | flops | bytes accessed | tf_op | source)
XLA Modules:
  0.0 1204.9 jit_solution(6223347452346712044)
XLA Ops:
  7.2 1.3 fusion.6
  8.5 1.3 iota_compare_fusion
  9.8 1.6 broadcast_select_fusion
  11.4 31.6 %all_to_all.20 = bf16[8,4,2048]{2,1,0:T(4,128)(2,1)S(1)} all-to-all(bf16[8,4,2048]{2,1,0:T(4,128)(2,1)S(1)} %get-tuple-element.159), channel_id=1, replica_groups=mesh['section'=8,'seq'=64] {'section'}, dimensions={0} | all-to-all | bytes 262144 | tf_op jit(solution)/shard_map/all_to_all | solution.py:39
  43.7 4.9 all-to-all-start.2
  48.6 3.3 copy.86
  52.6 1.3 dynamic-slice
  54.6 1.5 fusion.7
  56.1 6.4 all-to-all-done.2
  63.2 95.6 %all-gather.7.cloned.1.call-done = bf16[64,4,2048]{2,1,0:T(4,128)(2,1)} async-done(((bf16[1,4,2048]{2,1,0:T(4,128)(2,1)}), bf16[64,4,2048]{2,1,0:T(4,128)(2,1)}) %all-gather.7.cloned.1.call-update) | async-done | bytes 1048592 | tf_op jit(solution)/shard_map/all_gather | solution.py:45
  158.8 1.8 reshape.89
  161.4 1.8 fusion.8
  163.3 118.9 %all-gather = f32[512,256]{1,0:T(8,128)S(1)} all-gather(f32[8,256]{1,0:T(8,128)S(1)} %broadcast_maximum_fusion), channel_id=2, replica_groups=mesh['section'=8,'seq'=64] {'seq'}, dimensions={0}, use_global_device_ids=true | all-gather | bytes 532480 | tf_op jit(solution)/shard_map/all_gather | solution.py:11
  282.5 114.5 %all-gather.1 = f32[512,256]{1,0:T(8,128)S(1)} all-gather(f32[8,256]{1,0:T(8,128)S(1)} %exponential_reduce_fusion), channel_id=3, replica_groups=mesh['section'=8,'seq'=64] {'seq'}, dimensions={0}, use_global_device_ids=true | all-gather | bytes 532480 | tf_op jit(solution)/shard_map/all_gather | solution.py:11
  397.8 47.4 %while.17 = (s32[]{:T(128)}, f32[8,256]{1,0:T(8,128)S(1)}, f32[8,256]{1,0:T(8,128)S(1)}, f32[64,8,256]{2,1,0:T(8,128)}, f32[64,8,256]{2,1,0:T(8,128)}, /*index=5*/s32[]{:T(128)}, s32[]{:T(128)}, s32[]{:T(128)}) while((s32[]{:T(128)}, f32[8,256]{1,0:T(8,128)S(1)}, f32[8,256]{1,0:T(8,128)S(1)}, f32[64,8,256]{2,1,0:T(8,128)}, ...), condition=%wide.region_6.7_spmd, body=%wide.region_5.6_spmd.sunk | while | flops 12293 | bytes 49283 | solution.py:17
  445.3 2.6 reshape.93
  447.8 2.4 copy.100
  450.2 3.2 fusion.3
  453.5 2.0 multiply_reduce_fusion
  455.5 214.0 %psum.7 = f32[8,256]{1,0:T(8,128)S(1)} all-reduce(f32[8,256]{1,0:T(8,128)S(1)} %get-tuple-element.162), channel_id=1, replica_groups=mesh['section'=8,'seq'=64] {'seq'}, use_global_device_ids=true, to_apply=%region_11.12 | all-reduce | flops 2048 | bytes 16384 | tf_op jit(solution)/shard_map/psum | solution.py:78
  669.5 2.2 multiply_convert_fusion
  671.8 1.8 fusion.9
  673.6 470.9 %all-reduce.4 = (bf16[256,2048]{0,1:T(8,128)(2,1)}, bf16[256,2048]{0,1:T(8,128)(2,1)}) all-reduce(f32[256,2048]{0,1:T(8,128)} %bitcast.59, f32[256,2048]{0,1:T(8,128)} %bitcast.57), channel_id=4, replica_groups=mesh['section'=8,'seq'=64] {'seq'}, use_global_device_ids=true, to_apply=%region_7.8.clone | all-reduce | flops 1048576 | bytes 6291456
  1144.4 2.0 constant_dynamic-slice_fusion.1
  1147.7 2.1 constant_dynamic-slice_fusion
  1151.9 10.9 all-to-all-start.1
  1162.9 2.8 convolution_convert_fusion
  1165.7 2.4 copy.103
  1169.2 7.5 all-to-all-done.1
  1176.7 7.0 all-to-all-start.3
  1183.6 1.5 pad_maximum_fusion
  1185.7 11.7 all-to-all-done.3
  (99 shorter events, 55.2 us)
Async XLA Ops:
  7.2 151.7 %all-gather.7.cloned.1.call-start = ((), (), s32[]{:S(2)}) async-start(), calls=%async_computation.4 | async-start | bytes 1064960 | tf_op jit(solution)/shard_map/all_gather | solution.py:45
  43.7 18.8 %all-to-all-start.2 = ((bf16[8,4,2048]{2,1,0:T(4,128)(2,1)}), bf16[8,4,2048]{2,1,0:T(4,128)(2,1)S(1)}, u32[]{:S(2)}, u32[]{:S(2)}) async-start(bf16[8,4,2048]{2,1,0:T(4,128)(2,1)} %get-tuple-element.158), calls=%async_computation.2 | async-start | bytes 262144 | tf_op jit(solution)/shard_map/all_to_all | solution.py:40
  48.6 396.6 %all-gather.9.cloned.1.call-start = ((), (), s32[]{:S(2)}) async-start(), calls=%async_computation.5 | async-start | bytes 1064960 | tf_op jit(solution)/shard_map/all_gather | solution.py:46
  282.2 114.8 %copy-start.6 = (f32[512,256]{1,0:T(8,128)}, f32[512,256]{1,0:T(8,128)S(1)}, u32[]{:S(2)}) copy-start(f32[512,256]{1,0:T(8,128)S(1)} %all-gather) | copy-start | bytes 1572868
  397.0 0.8 copy-start.7
  450.2 3.2 copy-start.4
  450.2 3.2 copy-start.5
  669.5 2.2 copy-start.2
  671.7 1.8 copy-start
  1151.9 24.7 %all-to-all-start.1 = ((bf16[8,4,2048]{2,1,0:T(4,128)(2,1)}), bf16[8,4,2048]{2,1,0:T(4,128)(2,1)S(1)}, u32[]{:S(2)}, u32[]{:S(2)}) async-start(bf16[8,4,2048]{2,1,0:T(4,128)(2,1)} %get-tuple-element.157), calls=%async_computation.1 | async-start | bytes 262144 | tf_op jit(solution)/shard_map/all_to_all | solution.py:100
  1165.7 2.4 copy-start.1
  1168.5 15.1 %copy-start.3 = (bf16[1,256,2048]{2,1,0:T(8,128)(2,1)S(1)}, bf16[1,256,2048]{2,1,0:T(8,128)(2,1)}, u32[]{:S(2)}) copy-start(bf16[1,256,2048]{2,1,0:T(8,128)(2,1)} %copy.103) | copy-start | bytes 3145732
  1176.7 20.7 %all-to-all-start.3 = ((bf16[8,4,2048]{2,1,0:T(4,128)(2,1)}), bf16[8,4,2048]{2,1,0:T(4,128)(2,1)S(1)}, u32[]{:S(2)}, u32[]{:S(2)}) async-start(bf16[8,4,2048]{2,1,0:T(4,128)(2,1)} %get-tuple-element.156), calls=%async_computation.3 | async-start | bytes 262144 | tf_op jit(solution)/shard_map/all_to_all | solution.py:101
Sparse Core Ops, SparseCore 0:
  43.8 114.9 all-gather.6
  161.5 115.5 all-gather.8
where the time goes:
time: 1210 us; the launch traced here: 1200 us
  blocking collectives  950 us (79%)
  waiting for transfers between devices  121 us (10%)
  other arithmetic  57.8 us (5%)
  local copies, waits for them, and re-layouts  24.1 us (2%)
  starting transfers between devices  22.9 us (2%)
  between operations  15.5 us (1%)
  matrix products  12.1 us (1%)
    unnamed x1, blocking collectives  471 us
    all_gather x2, blocking collectives, combined_all(): everything = jax.tree.map(lambda part: lax.all_gather(part, axis), shard)  233 us
    psum x1, blocking collectives, shards(): delta = lax.psum(jnp.sum(probabilities * dprobs, axis=-1), 'seq')  214 us
    all_gather x1, waiting for transfers between devices, shards(): lax.all_gather(query_local, 'seq', axis=0, tiled=True)  95.6 us
    add x63, other arithmetic, combine_stats(): first[1] * jnp.exp(first[0] - top) + second[1] * jnp.exp(second[0] - top)  46.1 us
    all_to_all x1, blocking collectives, shards(): lax.all_to_all(query_send, 'section', split_axis=0, concat_axis=0, tiled=...  31.6 us
  transfers between devices with their start and end apart: 5, of which 4 were waited for; matrix products, arithmetic and copies ran while one was open for 5% of the time, Pallas kernels for 0%

commit v1 on v0

--- a/solution.py
+++ b/solution.py
@@ -5,6 +5,11 @@
 from jax.sharding import PartitionSpec as P
 
 HD = 256
+
+
+def add_all(x, name):
+    blocks = lax.all_gather(x, name)
+    return jnp.sum(blocks, axis=0)
 
 
 def combined_all(shard, axis, combine):
@@ -75,7 +80,7 @@
         tiled=True,
     )
     dprobs = jnp.einsum("ihd,jhd->hij", grad_heads, value_heads, preferred_element_type=jnp.float32)
-    delta = lax.psum(jnp.sum(probabilities * dprobs, axis=-1), "seq")
+    delta = add_all(jnp.sum(probabilities * dprobs, axis=-1), "seq")
     dscores = (probabilities * (dprobs - delta[..., None]) * score_scale).astype(jnp.bfloat16)
     result = jnp.einsum("hij,jhd->ihd", dscores, key_heads, preferred_element_type=jnp.float32)
     query_sum = lax.psum_scatter(

time: 1210 us -> 1110 us (0.917)
  blocking collectives: 950 us -> 852 us
    psum x1 -> x0, blocking collectives: 214 us -> none  [shards(): delta = lax.psum(jnp.sum(probabilities * dprobs, axis=-1), 'seq')]
    all_gather x0 -> x1, blocking collectives: none -> 116 us  [add_all(): blocks = lax.all_gather(x, name)]
  transfers between devices with their start and end apart: 5 -> 5, of which waited for: 4 -> 4; matrix products, arithmetic and copies ran while one was open for 5% -> 6% of each run, Pallas kernels for 0% -> 0%
where the time goes in v1:
time: 1110 us; the launch traced here: 1100 us
  blocking collectives  852 us (77%)
  waiting for transfers between devices  121 us (11%)
  other arithmetic  56.2 us (5%)
  local copies, waits for them, and re-layouts  24.7 us (2%)
  starting transfers between devices  22.7 us (2%)
  between operations  15.5 us (1%)
    unnamed x1, blocking collectives  471 us
    all_gather x2, blocking collectives, combined_all(): everything = jax.tree.map(lambda part: lax.all_gather(part, axis), shard)  233 us
    all_gather x1, blocking collectives, add_all(): blocks = lax.all_gather(x, name)  116 us
    all_gather x1, waiting for transfers between devices, shards(): lax.all_gather(query_local, 'seq', axis=0, tiled=True)  95.6 us
    add x63, other arithmetic, combine_stats(): first[1] * jnp.exp(first[0] - top) + second[1] * jnp.exp(second[0] - top)  46.1 us
    all_to_all x1, blocking collectives, shards(): lax.all_to_all(query_send, 'section', split_axis=0, concat_axis=0, tiled=...  31.6 us
  transfers between devices with their start and end apart: 5, of which 4 were waited for; matrix products, arithmetic and copies ran while one was open for 6% of the time, Pallas kernels for 0%

profile of v1, /device:TPU:2, one launch (start us, length us, event | category | flops | bytes accessed | tf_op | source)
XLA Modules:
  0.0 1104.9 jit_solution(12918390950696734801)
XLA Ops:
  7.2 1.3 fusion.6
  8.5 1.3 iota_compare_fusion
  9.8 1.6 broadcast_select_fusion
  11.4 31.6 %all_to_all.20 = bf16[8,4,2048]{2,1,0:T(4,128)(2,1)S(1)} all-to-all(bf16[8,4,2048]{2,1,0:T(4,128)(2,1)S(1)} %get-tuple-element.159), channel_id=1, replica_groups=mesh['section'=8,'seq'=64] {'section'}, dimensions={0} | all-to-all | bytes 262144 | tf_op jit(solution)/shard_map/all_to_all | solution.py:44
  43.7 4.9 all-to-all-start.2
  48.6 3.3 copy.86
  52.6 1.3 dynamic-slice
  54.6 1.5 fusion.7
  56.1 6.4 all-to-all-done.2
  63.2 95.6 %all-gather.8.cloned.1.call-done = bf16[64,4,2048]{2,1,0:T(4,128)(2,1)} async-done(((bf16[1,4,2048]{2,1,0:T(4,128)(2,1)}), bf16[64,4,2048]{2,1,0:T(4,128)(2,1)}) %all-gather.8.cloned.1.call-update) | async-done | bytes 1048592 | tf_op jit(solution)/shard_map/all_gather | solution.py:50
  158.8 1.8 reshape.89
  161.4 1.8 fusion.8
  163.3 118.9 %all-gather = f32[512,256]{1,0:T(8,128)S(1)} all-gather(f32[8,256]{1,0:T(8,128)S(1)} %broadcast_maximum_fusion), channel_id=2, replica_groups=mesh['section'=8,'seq'=64] {'seq'}, dimensions={0}, use_global_device_ids=true | all-gather | bytes 532480 | tf_op jit(solution)/shard_map/all_gather | solution.py:16
  282.5 114.5 %all-gather.1 = f32[512,256]{1,0:T(8,128)S(1)} all-gather(f32[8,256]{1,0:T(8,128)S(1)} %exponential_reduce_fusion), channel_id=3, replica_groups=mesh['section'=8,'seq'=64] {'seq'}, dimensions={0}, use_global_device_ids=true | all-gather | bytes 532480 | tf_op jit(solution)/shard_map/all_gather | solution.py:16
  397.8 47.4 %while.17 = (s32[]{:T(128)}, f32[8,256]{1,0:T(8,128)S(1)}, f32[8,256]{1,0:T(8,128)S(1)}, f32[64,8,256]{2,1,0:T(8,128)}, f32[64,8,256]{2,1,0:T(8,128)}, /*index=5*/s32[]{:T(128)}, s32[]{:T(128)}, s32[]{:T(128)}) while((s32[]{:T(128)}, f32[8,256]{1,0:T(8,128)S(1)}, f32[8,256]{1,0:T(8,128)S(1)}, f32[64,8,256]{2,1,0:T(8,128)}, ...), condition=%wide.region_6.7_spmd, body=%wide.region_5.6_spmd.sunk | while | flops 12293 | bytes 49283 | solution.py:22
  445.3 2.6 reshape.93
  447.8 2.4 copy.100
  450.2 3.2 fusion.3
  454.3 116.0 %all-gather.2 = f32[512,256]{1,0:T(8,128)S(1)} all-gather(f32[8,256]{1,0:T(8,128)S(1)} %get-tuple-element.162), channel_id=4, replica_groups=mesh['section'=8,'seq'=64] {'seq'}, dimensions={0}, use_global_device_ids=true | all-gather | bytes 532480 | tf_op jit(solution)/shard_map/all_gather | solution.py:11
  571.5 1.8 fusion.9
  573.3 471.3 %all-reduce.4 = (bf16[256,2048]{0,1:T(8,128)(2,1)}, bf16[256,2048]{0,1:T(8,128)(2,1)}) all-reduce(f32[256,2048]{0,1:T(8,128)} %bitcast.61, f32[256,2048]{0,1:T(8,128)} %bitcast.59), channel_id=5, replica_groups=mesh['section'=8,'seq'=64] {'seq'}, use_global_device_ids=true, to_apply=%region_7.8.clone | all-reduce | flops 1048576 | bytes 6291456
  1044.6 2.0 constant_dynamic-slice_fusion.1
  1046.7 1.2 copy.90
  1047.9 2.1 constant_dynamic-slice_fusion
  1050.0 1.2 copy.96
  1052.1 10.7 all-to-all-start.1
  1062.8 2.8 convolution_convert_fusion
  1065.6 2.4 copy.103
  1069.1 7.5 all-to-all-done.1
  1076.6 7.0 all-to-all-start.3
  1083.6 1.5 pad_maximum_fusion
  1085.7 11.7 %all-to-all-done.3 = bf16[8,4,2048]{2,1,0:T(4,128)(2,1)S(1)} async-done(((bf16[8,4,2048]{2,1,0:T(4,128)(2,1)}), bf16[8,4,2048]{2,1,0:T(4,128)(2,1)S(1)}, u32[]{:S(2)}, u32[]{:S(2)}) %all-to-all-start.3) | async-done | bytes 131104 | tf_op jit(solution)/shard_map/all_to_all | solution.py:106
  (100 shorter events, 54.8 us)
Async XLA Ops:
  7.2 151.7 %all-gather.8.cloned.1.call-start = ((), (), s32[]{:S(2)}) async-start(), calls=%async_computation.4 | async-start | bytes 1064960 | tf_op jit(solution)/shard_map/all_gather | solution.py:50
  43.7 18.8 %all-to-all-start.2 = ((bf16[8,4,2048]{2,1,0:T(4,128)(2,1)}), bf16[8,4,2048]{2,1,0:T(4,128)(2,1)S(1)}, u32[]{:S(2)}, u32[]{:S(2)}) async-start(bf16[8,4,2048]{2,1,0:T(4,128)(2,1)} %get-tuple-element.158), calls=%async_computation.2 | async-start | bytes 262144 | tf_op jit(solution)/shard_map/all_to_all | solution.py:45
  48.6 396.6 %all-gather.10.cloned.1.call-start = ((), (), s32[]{:S(2)}) async-start(), calls=%async_computation.5 | async-start | bytes 1064960 | tf_op jit(solution)/shard_map/all_gather | solution.py:51
  282.2 114.8 %copy-start.6 = (f32[512,256]{1,0:T(8,128)}, f32[512,256]{1,0:T(8,128)S(1)}, u32[]{:S(2)}) copy-start(f32[512,256]{1,0:T(8,128)S(1)} %all-gather) | copy-start | bytes 1572868
  397.0 0.8 copy-start.7
  450.2 3.2 copy-start.4
  450.2 3.2 copy-start.5
  570.3 1.2 copy-start.2
  571.5 1.8 copy-start
  1052.1 24.5 %all-to-all-start.1 = ((bf16[8,4,2048]{2,1,0:T(4,128)(2,1)}), bf16[8,4,2048]{2,1,0:T(4,128)(2,1)S(1)}, u32[]{:S(2)}, u32[]{:S(2)}) async-start(bf16[8,4,2048]{2,1,0:T(4,128)(2,1)} %get-tuple-element.157), calls=%async_computation.1 | async-start | bytes 262144 | tf_op jit(solution)/shard_map/all_to_all | solution.py:105
  1065.6 2.4 copy-start.1
  1068.5 15.1 %copy-start.3 = (bf16[1,256,2048]{2,1,0:T(8,128)(2,1)S(1)}, bf16[1,256,2048]{2,1,0:T(8,128)(2,1)}, u32[]{:S(2)}) copy-start(bf16[1,256,2048]{2,1,0:T(8,128)(2,1)} %copy.103) | copy-start | bytes 3145732
  1076.6 20.7 %all-to-all-start.3 = ((bf16[8,4,2048]{2,1,0:T(4,128)(2,1)}), bf16[8,4,2048]{2,1,0:T(4,128)(2,1)S(1)}, u32[]{:S(2)}, u32[]{:S(2)}) async-start(bf16[8,4,2048]{2,1,0:T(4,128)(2,1)} %get-tuple-element.156), calls=%async_computation.3 | async-start | bytes 262144 | tf_op jit(solution)/shard_map/all_to_all | solution.py:106
Sparse Core Ops, SparseCore 0:
  43.8 114.9 all-gather.7
  161.5 115.5 all-gather.9
